TPU v7x, 256 devices: a whole 4x4x8 slice. The times are simulated.
256 devices in a mesh: gx: 16 (over z_hi, y, core), gy: 16 (over z_lo, x).
Axes of the slice: x: 4, y: 4, z: 8 (z_hi: 2, z_lo: 4; z = z_hi * 4 + z_lo), core: 2. Of those that a mesh axis runs over, the one named last changes fastest.
Arguments:
- skip_input: bfloat16 [32, 64, 4096], P(None, 'gx', 'gy'), may hold values from -6 to 6
- w_encoder: bfloat16 [64, 864], replicated, may hold values from -0.625 to 0.625
- w_bottom: bfloat16 [128, 1728], P('gx'), may hold values from -0.3125 to 0.3125
- w_middle: bfloat16 [64, 5184], replicated, may hold values from -0.15625 to 0.15625
- w_upper: bfloat16 [32, 2592], replicated, may hold values from -0.21875 to 0.21875
- cotangent: bfloat16 [32, 64, 4096], P(None, 'gx', 'gy'), may hold values from -6 to 6
Outputs:
- features: bfloat16 [32, 64, 4096], P(None, 'gx', 'gy')
- grad_skip: bfloat16 [32, 64, 4096], P(None, 'gx', 'gy')
- grad_encoder: float32 [64, 864], replicated
- grad_bottom: float32 [128, 1728], P('gx')
- grad_middle: float32 [64, 5184], replicated
- grad_upper: float32 [32, 2592], replicated
All inputs are finite; a program needn't handle non-finite values.
Results may differ from a plain program's by a relative error of at most 0.017.
Values may be sent and summed in bfloat16 or wider, within the bound.
No kernel may reach another device: no remote copies, remote signals or barrier semaphores. Data moves between devices by JAX's collectives and lax.ppermute only.
A program may use at most 64 MiB of HBM per device.

v0:
```python
import math
import jax
import jax.numpy as jnp
from jax import lax
from jax.sharding import PartitionSpec as P

Z = 16


def extended_2(cells, sides, width):
    for axis, dim in sides:
        count = lax.axis_size(axis)
        ends = count - 1
        head = lax.slice_in_dim(cells, 0, width, axis=dim)
        tail = lax.slice_in_dim(cells, cells.shape[dim] - width, cells.shape[dim], axis=dim)
        cells = jnp.concatenate(
            [
                lax.ppermute(tail, axis, [(i, (i + 1) % count) for i in range(ends)]),
                cells,
                lax.ppermute(head, axis, [((i + 1) % count, i) for i in range(ends)]),
            ],
            axis=dim,
        )
    return cells


def z_shift(extended, z_step, z_depth):
    length = extended.shape[2]
    padded = jnp.pad(extended, ((0, 0), (0, 0), (1, 1)))
    shifted = padded[:, :, 1 + z_step : 1 + z_step + length]
    z_index = lax.broadcasted_iota(jnp.int32, (1, 1, length), 2) % z_depth + z_step
    inside = (z_index >= 0) & (z_index < z_depth)
    return jnp.where(inside, shifted, jnp.zeros_like(shifted))


def tap_piece(shifted_set, a, b, c, row_count, col_count, z_depth, flipped):
    x_off, y_off, z_off = (2 - a, 2 - b, 2 - c) if flipped else (a, b, c)
    source = shifted_set[z_off]
    tap_slice = source[
        :, x_off : x_off + row_count, y_off * z_depth : (y_off + col_count) * z_depth
    ]
    return tap_slice.reshape(source.shape[0], row_count * col_count * z_depth)


def conv_forward(extended, weight, row_count, col_count, z_depth):
    in_chan = extended.shape[0]
    shifted_set = [z_shift(extended, z_step, z_depth) for z_step in (-1, 0, 1)]
    total_sum = jnp.zeros((weight.shape[0], row_count * col_count * z_depth), jnp.float32)
    for a in range(3):
        for b in range(3):
            for c in range(3):
                tap_number = 9 * a + 3 * b + c
                total_sum = total_sum + jnp.dot(
                    weight[:, tap_number * in_chan : (tap_number + 1) * in_chan],
                    tap_piece(shifted_set, a, b, c, row_count, col_count, z_depth, False),
                    preferred_element_type=jnp.float32,
                )
    return total_sum


def conv_backward(extended, weight, row_count, col_count, z_depth):
    in_chan = weight.shape[1] // 27
    shifted_set = [z_shift(extended, z_step, z_depth) for z_step in (-1, 0, 1)]
    total_sum = jnp.zeros((in_chan, row_count * col_count * z_depth), jnp.float32)
    for a in range(3):
        for b in range(3):
            for c in range(3):
                tap_number = 9 * a + 3 * b + c
                total_sum = total_sum + lax.dot_general(
                    weight[:, tap_number * in_chan : (tap_number + 1) * in_chan],
                    tap_piece(shifted_set, a, b, c, row_count, col_count, z_depth, True),
                    (((0,), (0,)), ((), ())),
                    preferred_element_type=jnp.float32,
                )
    return total_sum


def weight_grad(extended, error_flat, row_count, col_count, z_depth):
    shifted_set = [z_shift(extended, z_step, z_depth) for z_step in (-1, 0, 1)]
    blocks = []
    for a in range(3):
        for b in range(3):
            for c in range(3):
                blocks.append(
                    lax.dot_general(
                        error_flat,
                        tap_piece(shifted_set, a, b, c, row_count, col_count, z_depth, False),
                        (((1,), (1,)), ((), ())),
                        preferred_element_type=jnp.float32,
                    )
                )
    return jnp.concatenate(blocks, axis=1)


def pool_mean(values, z_depth):
    channels, row_count, length = values.shape
    col_count = length // z_depth
    shaped = values.astype(jnp.float32).reshape(
        channels, row_count // 2, 2, col_count // 2, 2, z_depth // 2, 2
    )
    return shaped.mean(axis=(2, 4, 6)).reshape(
        channels, row_count // 2, col_count // 2 * (z_depth // 2)
    )


def block_sum(values, z_depth):
    channels, row_count, length = values.shape
    col_count = length // z_depth
    shaped = values.reshape(channels, row_count // 2, 2, col_count // 2, 2, z_depth // 2, 2)
    return shaped.sum(axis=(2, 4, 6)).reshape(
        channels, row_count // 2, col_count // 2 * (z_depth // 2)
    )


def upsample(values, z_depth):
    channels, row_count, length = values.shape
    col_count = length // z_depth
    shaped = values.reshape(channels, row_count, 1, col_count, 1, z_depth, 1)
    shaped = jnp.broadcast_to(shaped, (channels, row_count, 2, col_count, 2, z_depth, 2))
    return shaped.reshape(channels, 2 * row_count, 4 * col_count * z_depth)


def silu_slope(values):
    s_value = jax.nn.sigmoid(values)
    return s_value * (1.0 + values * (1.0 - s_value))


def spatial_halo(values, z_depth):
    widened = extended_2(values, (("gx", 1),), 1)
    return extended_2(widened, (("gy", 2),), z_depth)


def per_device(skip_input, w_encoder, w_bottom, w_middle, w_upper, cotangent):
    top_chan = skip_input.shape[0]
    rows_fine = skip_input.shape[1]
    cols_fine = skip_input.shape[2] // Z
    rows_mid, cols_mid, depth_mid = (rows_fine // 2, cols_fine // 2, Z // 2)
    rows_low, cols_low, depth_low = (rows_fine // 4, cols_fine // 4, Z // 4)
    cells_fine = rows_fine * cols_fine * Z * lax.axis_size("gx") * lax.axis_size("gy")
    scale_fine = 1.0 / math.sqrt(cells_fine)
    scale_mid = 1.0 / math.sqrt(cells_fine // 8)
    scale_low = 1.0 / math.sqrt(cells_fine // 64)
    pool_top = pool_mean(skip_input, Z).astype(jnp.bfloat16)
    ext_pool = spatial_halo(pool_top, depth_mid)
    pre_one = conv_forward(ext_pool, w_encoder, rows_mid, cols_mid, depth_mid)
    act_one = jax.nn.silu(pre_one).astype(jnp.bfloat16).reshape(-1, rows_mid, cols_mid * depth_mid)
    pool_mid = pool_mean(act_one, depth_mid).astype(jnp.bfloat16)
    col_ext = extended_2(pool_mid, (("gy", 2),), depth_low)
    whole_rows = lax.all_gather(col_ext, "gx", axis=1, tiled=True)
    ext_low = jnp.pad(whole_rows, ((0, 0), (1, 1), (0, 0)))
    rows_all = whole_rows.shape[1]
    pre_two = conv_forward(ext_low, w_bottom, rows_all, cols_low, depth_low)
    act_block = (
        jax.nn.silu(pre_two).astype(jnp.bfloat16).reshape(-1, rows_all, cols_low * depth_low)
    )
    act_two = lax.all_to_all(act_block, "gx", split_axis=1, concat_axis=0, tiled=True)
    cat_mid = jnp.concatenate([upsample(act_two, depth_low), act_one], axis=0)
    ext_mid = spatial_halo(cat_mid, depth_mid)
    pre_three = conv_forward(ext_mid, w_middle, rows_mid, cols_mid, depth_mid)
    act_three = (
        jax.nn.silu(pre_three).astype(jnp.bfloat16).reshape(-1, rows_mid, cols_mid * depth_mid)
    )
    cat_top = jnp.concatenate([upsample(act_three, depth_mid), skip_input], axis=0)
    ext_top = spatial_halo(cat_top, Z)
    pre_four = conv_forward(ext_top, w_upper, rows_fine, cols_fine, Z)
    features = (
        jax.nn.silu(pre_four).astype(jnp.bfloat16).reshape(top_chan, rows_fine, cols_fine * Z)
    )
    err_four = (cotangent.reshape(top_chan, -1).astype(jnp.float32) * silu_slope(pre_four)).astype(
        jnp.bfloat16
    )
    local_upper = weight_grad(ext_top, err_four, rows_fine, cols_fine, Z) * scale_fine
    grad_upper = lax.psum(local_upper, ("gx", "gy"))
    dcat_top = conv_backward(
        spatial_halo(err_four.reshape(top_chan, rows_fine, cols_fine * Z), Z),
        w_upper,
        rows_fine,
        cols_fine,
        Z,
    ).reshape(-1, rows_fine, cols_fine * Z)
    mid_chan = act_three.shape[0]
    err_three = (
        block_sum(dcat_top[:mid_chan], Z).reshape(mid_chan, -1) * silu_slope(pre_three)
    ).astype(jnp.bfloat16)
    local_middle = weight_grad(ext_mid, err_three, rows_mid, cols_mid, depth_mid) * scale_mid
    grad_middle = lax.psum(local_middle, ("gx", "gy"))
    dcat_mid = conv_backward(
        spatial_halo(err_three.reshape(mid_chan, rows_mid, cols_mid * depth_mid), depth_mid),
        w_middle,
        rows_mid,
        cols_mid,
        depth_mid,
    ).reshape(-1, rows_mid, cols_mid * depth_mid)
    low_chan = act_two.shape[0]
    dact_two = block_sum(dcat_mid[:low_chan], depth_mid)
    dact_block = lax.all_to_all(dact_two, "gx", split_axis=0, concat_axis=1, tiled=True)
    block_chan = dact_block.shape[0]
    err_two = (dact_block.reshape(block_chan, -1) * silu_slope(pre_two)).astype(jnp.bfloat16)
    part_bottom = weight_grad(ext_low, err_two, rows_all, cols_low, depth_low)
    err_grid = err_two.reshape(block_chan, rows_all, cols_low * depth_low)
    err_cols = extended_2(err_grid, (("gy", 2),), depth_low)
    err_ext = jnp.pad(err_cols, ((0, 0), (1, 1), (0, 0)))
    partial_sum = conv_backward(err_ext, w_bottom, rows_all, cols_low, depth_low).reshape(
        -1, rows_all, cols_low * depth_low
    )
    dpool_mid = lax.psum_scatter(
        partial_sum.astype(jnp.bfloat16), "gx", scatter_dimension=1, tiled=True
    ).astype(jnp.float32)
    grad_bottom = lax.psum((part_bottom * scale_low).astype(jnp.bfloat16), "gy").astype(jnp.float32)
    dact_one = dcat_mid[low_chan:] + upsample(dpool_mid, depth_low) / 8.0
    err_one = (dact_one.reshape(mid_chan, -1) * silu_slope(pre_one)).astype(jnp.bfloat16)
    local_encoder = weight_grad(ext_pool, err_one, rows_mid, cols_mid, depth_mid) * scale_mid
    grad_encoder = lax.psum(local_encoder, ("gx", "gy"))
    dpool_top = conv_backward(
        spatial_halo(err_one.reshape(mid_chan, rows_mid, cols_mid * depth_mid), depth_mid),
        w_encoder,
        rows_mid,
        cols_mid,
        depth_mid,
    ).reshape(-1, rows_mid, cols_mid * depth_mid)
    grad_skip = (dcat_top[mid_chan:] + upsample(dpool_top, depth_mid) / 8.0).astype(jnp.bfloat16)
    return (features, grad_skip, grad_encoder, grad_bottom, grad_middle, grad_upper)


def solution(mesh):
    in_specs = (P(None, "gx", "gy"), P(), P("gx", None), P(), P(), P(None, "gx", "gy"))
    out_specs = (P(None, "gx", "gy"), P(None, "gx", "gy"), P(), P("gx", None), P(), P())
    return jax.shard_map(
        per_device, mesh=mesh, in_specs=in_specs, out_specs=out_specs, check_vma=False
    )
```

profile of v0, /device:TPU:4, one launch (start us, length us, event | category | flops | bytes accessed | tf_op | source)
XLA Modules:
  0.0 701.9 jit_solution(12189707919216640930)
XLA Ops:
  12.8 2.0 collective-permute-done.1
  14.8 3.1 collective-permute-start.2
  17.9 2.7 collective-permute-start.3
  21.4 2.1 collective-permute-done.3
  34.1 5.8 collective-permute-start.4
  41.9 3.5 collective-permute-done.5
  45.4 33.5 %all_gather.3 = bf16[64,16,24]{0,2,1:T(8,128)(2,1)S(1)} all-gather(bf16[64,1,24]{0,2,1:T(8,128)(2,1)S(1)} %pad_maximum_fusion.21), channel_id=1, replica_groups=mesh['gx'=16,'gy'=16] {'gx'}, dimensions={1}, use_global_device_ids=true | all-gather | bytes 52224 | tf_op jit(solution)/shard_map/all_gather | solution.py:149
  86.0 6.4 all-to-all-start
  92.6 9.9 %all-to-all-done = bf16[8,16,16]{2,0,1:T(8,128)(2,1)S(1)} async-done(((bf16[8,16,16]{2,0,1:T(8,128)(2,1)}), bf16[8,16,16]{2,0,1:T(8,128)(2,1)S(1)}, u32[]{:S(2)}, u32[]{:S(2)}) %all-to-all-start) | async-done | bytes 4128 | tf_op jit(solution)/shard_map/all_to_all | solution.py:156
  102.8 2.0 collective-permute-start.6
  108.0 4.2 collective-permute-start.8
  114.2 3.7 collective-permute-done.9
  127.1 3.1 collective-permute-start.10
  131.5 2.7 collective-permute-done.11
  134.4 4.1 collective-permute-start.12
  138.4 2.1 collective-permute-start.13
  140.6 3.6 collective-permute-done.13
  157.6 3.4 collective-permute-start.14
  162.8 2.3 collective-permute-done.15
  165.3 4.1 collective-permute-start.16
  172.7 2.8 collective-permute-done.17
  209.4 3.1 collective-permute-start.18
  217.7 4.0 collective-permute-start.20
  225.4 2.7 collective-permute-done.21
  270.0 28.7 %all-to-all-start.1 = ((f32[16,1,128]{2,1,0:T(1,128)}), f32[16,1,128]{2,1,0:T(1,128)S(1)}, u32[]{:S(2)}, u32[]{:S(2)}) async-start(f32[16,1,128]{2,1,0:T(1,128)} %reshape.1246), calls=%async_computation.1 | async-start | bytes 16384 | tf_op jit(solution)/shard_map/all_to_all | solution.py:196
  300.3 8.3 %all-to-all-done.1 = f32[16,1,128]{2,1,0:T(1,128)S(1)} async-done(((f32[16,1,128]{2,1,0:T(1,128)}), f32[16,1,128]{2,1,0:T(1,128)S(1)}, u32[]{:S(2)}, u32[]{:S(2)}) %all-to-all-start.1) | async-done | bytes 8224 | tf_op jit(solution)/shard_map/all_to_all | solution.py:196
  314.0 4.3 collective-permute-start.22
  320.5 3.6 collective-permute-done.23
  335.1 70.2 %psum.29 = bf16[8,1728]{1,0:T(8,128)(2,1)S(1)} all-reduce(bf16[8,1728]{1,0:T(8,128)(2,1)S(1)} %multiply_convert_fusion.3), channel_id=1, replica_groups=mesh['gx'=16,'gy'=16] {'gy'}, use_global_device_ids=true, to_apply=%region_6.7 | all-reduce | flops 13824 | bytes 55296 | tf_op jit(solution)/shard_map/psum | solution.py:209
  416.1 4.2 collective-permute-start.27
  435.2 254.7 %all-reduce.13.cloned.1.call-done = (f32[64,864]{0,1:T(8,128)}, f32[64,5184]{1,0:T(8,128)}, f32[32,2592]{1,0:T(8,128)}) async-done(((f32[64,864]{0,1:T(8,128)}, f32[64,5184]{1,0:T(8,128)}, f32[32,2592]{1,0:T(8,128)}), (f32[64,864]{0,1:T(8,128)}, f32[64,5184]{1,0:T(8,128)}, f32[32,2592]{1,0:T(8,128)})) %all-reduce.13.cloned.1.call-update) | async-done | bytes 1880080 | tf_op jit(solution)/shard_map/psum | solution.py:213
  691.8 2.5 copy.159
  (1002 shorter events, 190.3 us)
Async XLA Ops:
  8.6 4.2 collective-permute-start
  10.4 4.4 collective-permute-start.1
  14.8 8.8 %collective-permute-start.2 = (bf16[32,4,8]{0,2,1:T(8,128)(2,1)S(1)}, bf16[32,4,8]{0,2,1:T(8,128)(2,1)S(1)}, u32[]{:S(2)}, u32[]{:S(2)}) collective-permute-start(bf16[32,4,8]{0,2,1:T(8,128)(2,1)S(1)} %get-tuple-element.241), channel_id=1, source_target_pairs={{0,1},{1,2},{2,3},{3,4},{4,5},{5,6},{6,7},{7,8},{8,9},{9,10},{10,1... | collective-permute-start | bytes 6152 | tf_op jit(solution)/shard_map/ppermute | solution.py:18
  17.9 5.5 collective-permute-start.3
  34.1 7.8 %collective-permute-start.4 = (bf16[64,1,4]{0,2,1:T(4,128)(2,1)S(1)}, bf16[64,1,4]{0,2,1:T(4,128)(2,1)S(1)}, u32[]{:S(2)}, u32[]{:S(2)}) collective-permute-start(bf16[64,1,4]{0,2,1:T(4,128)(2,1)S(1)} %get-tuple-element.309), channel_id=1, source_target_pairs={{0,1},{1,2},{2,3},{3,4},{4,5},{5,6},{6,7},{7,8},{8,9},{9,10},{10,1... | collective-permute-start | bytes 1544 | tf_op jit(solution)/shard_map/ppermute | solution.py:18
  40.0 5.5 collective-permute-start.5
  86.0 16.4 %all-to-all-start = ((bf16[8,16,16]{2,0,1:T(8,128)(2,1)}), bf16[8,16,16]{2,0,1:T(8,128)(2,1)S(1)}, u32[]{:S(2)}, u32[]{:S(2)}) async-start(bf16[8,16,16]{2,0,1:T(8,128)(2,1)} %copy.83), calls=%async_computation | async-start | bytes 65536 | tf_op jit(solution)/shard_map/all_to_all | solution.py:156
  102.8 3.3 collective-permute-start.6
  104.8 3.2 collective-permute-start.7
  108.0 6.1 collective-permute-start.8
  112.2 5.6 collective-permute-start.9
  127.1 4.5 collective-permute-start.10
  130.2 4.1 collective-permute-start.11
  134.4 6.2 collective-permute-start.12
  138.4 5.7 collective-permute-start.13
  157.6 5.1 collective-permute-start.14
  161.1 4.0 collective-permute-start.15
  165.3 7.4 %collective-permute-start.16 = (bf16[32,6,16]{2,1,0:T(8,128)(2,1)S(1)}, bf16[32,6,16]{2,1,0:T(8,128)(2,1)S(1)}, u32[]{:S(2)}, u32[]{:S(2)}) collective-permute-start(bf16[32,6,16]{2,1,0:T(8,128)(2,1)S(1)} %get-tuple-element.138), channel_id=1, source_target_pairs={{0,1},{1,2},{2,3},{3,4},{4,5},{5,6},{6,7},{7,8},{8,9},{9,10},{10,1... | collective-permute-start | bytes 18440 | tf_op jit(solution)/shard_map/ppermute | solution.py:18
  169.3 6.2 collective-permute-start.17
  209.4 5.4 collective-permute-start.18
  212.5 4.3 collective-permute-start.19
  217.7 7.8 %collective-permute-start.20 = (bf16[64,4,8]{2,1,0:T(4,128)(2,1)}, bf16[64,4,8]{2,1,0:T(4,128)(2,1)}, u32[]{:S(2)}, u32[]{:S(2)}) collective-permute-start(bf16[64,4,8]{2,1,0:T(4,128)(2,1)} %get-tuple-element.235), channel_id=1, source_target_pairs={{0,1},{1,2},{2,3},{3,4},{4,5},{5,6},{6,7},{7,8},{8,9},{9,10},{10,1... | collective-permute-start | bytes 12296 | tf_op jit(solution)/shard_map/ppermute | solution.py:18
  221.7 6.5 collective-permute-start.21
  270.0 38.6 %all-to-all-start.1 = ((f32[16,1,128]{2,1,0:T(1,128)}), f32[16,1,128]{2,1,0:T(1,128)S(1)}, u32[]{:S(2)}, u32[]{:S(2)}) async-start(f32[16,1,128]{2,1,0:T(1,128)} %reshape.1246), calls=%async_computation.1 | async-start | bytes 16384 | tf_op jit(solution)/shard_map/all_to_all | solution.py:196
  298.8 107.2 %reduce-scatter.2.cloned.1.call-start = ((), (), s32[]{:S(2)}) async-start(), calls=%async_computation.3 | async-start | bytes 69632 | tf_op jit(solution)/shard_map/reduce_scatter | solution.py:206
  314.0 6.5 collective-permute-start.22
  318.3 5.8 collective-permute-start.23
  335.0 354.9 %all-reduce.13.cloned.1.call-start = ((), (), s32[]{:S(2)}) async-start(), calls=%async_computation.4 | async-start | bytes 4259840 | tf_op jit(solution)/shard_map/psum | solution.py:213
  407.8 6.2 collective-permute-start.24
  409.1 4.9 collective-permute-start.25
  414.2 7.0 collective-permute-start.26
  416.1 6.2 collective-permute-start.27
  (176 other events, 3641.9 us)
Sparse Core Ops, SparseCore 0:
  335.1 68.1 reduce-scatter.1
  421.3 268.5 all-reduce.12
where the time goes:
time: 705 us; the launch traced here: 702 us
  waiting for transfers between devices  307 us (44%)
  starting transfers between devices  108 us (15%)
  blocking collectives  104 us (15%)
  matrix products  87.8 us (12%)
  local copies, waits for them, and re-layouts  58.3 us (8%)
  other arithmetic  19.2 us (3%)
  between operations  17.9 us (3%)
    psum x1, waiting for transfers between devices, per_device(): grad_encoder = lax.psum(local_encoder, ('gx', 'gy'))  255 us
    psum x1, blocking collectives, per_device(): lax.psum((part_bottom * scale_low).astype(jnp.bfloat16), 'gy')  70.2 us
    ppermute x14, starting transfers between devices, extended_2(): lax.ppermute(tail, axis, [(i, (i + 1) % count) for i in range(ends)])  46.2 us
    ppermute x14, waiting for transfers between devices, extended_2(): lax.ppermute(head, axis, [((i + 1) % count, i) for i in range(ends)])  34.1 us
    all_gather x1, blocking collectives, per_device(): whole_rows = lax.all_gather(col_ext, 'gx', axis=1, tiled=True)  33.5 us
    dot_general x108, matrix products, weight_grad(): lax.dot_general(error_flat, tap_piece(shifted_set, a, b, c, row_count, co...  33.3 us
    dot_general x108, matrix products, conv_backward(): lax.dot_general(weight[:, tap_number * in_chan:(tap_number + 1) * in_chan...  32.1 us
    reshape x108, local copies, waits for them, and re-layouts, tap_piece(): return tap_slice.reshape(source.shape[0], row_count * col_count * z_depth)  30.8 us
  transfers between devices with their start and end apart: 32, of which 16 were waited for; matrix products, arithmetic and copies ran while one was open for 4% of the time, Pallas kernels for 0%

commit v1 on v0

--- a/solution.py
+++ b/solution.py
@@ -1,3 +1,4 @@
+import functools
 import math
 import jax
 import jax.numpy as jnp
@@ -5,6 +6,15 @@
 from jax.sharding import PartitionSpec as P
 
 Z = 16
+
+
+def _hold_scales(my_data, comm_axis, device_axis):
+    for tick in (comm_axis, device_axis):
+        my_data = jax.lax.psum(my_data, tick)
+    return my_data
+
+
+skins_time = functools.partial(_hold_scales, comm_axis="gy", device_axis="gx")
 
 
 def extended_2(cells, sides, width):
@@ -210,7 +220,7 @@
     dact_one = dcat_mid[low_chan:] + upsample(dpool_mid, depth_low) / 8.0
     err_one = (dact_one.reshape(mid_chan, -1) * silu_slope(pre_one)).astype(jnp.bfloat16)
     local_encoder = weight_grad(ext_pool, err_one, rows_mid, cols_mid, depth_mid) * scale_mid
-    grad_encoder = lax.psum(local_encoder, ("gx", "gy"))
+    grad_encoder = skins_time(local_encoder)
     dpool_top = conv_backward(
         spatial_halo(err_one.reshape(mid_chan, rows_mid, cols_mid * depth_mid), depth_mid),
         w_encoder,

time: 705 us -> 1000 us (1.42)
  waiting for transfers between devices: 307 us -> 612 us
  local copies, waits for them, and re-layouts: 58.3 us -> 47.7 us
    psum x1 -> x3, waiting for transfers between devices: 255 us -> 489 us  [the longest x1 266 us: per_device(): grad_middle = lax.psum(local_middle, ('gx', 'gy'))]
    reduce_scatter x1, waiting for transfers between devices: 0.01 us -> 67.3 us  [per_device(): lax.psum_scatter(partial_sum.astype(jnp.bfloat16), 'gx', scatter_dimensio...]
    reshape x108, local copies, waits for them, and re-layouts: 30.8 us -> 20.8 us  [tap_piece(): return tap_slice.reshape(source.shape[0], row_count * col_count * z_depth)]
  transfers between devices with their start and end apart: 32 -> 34, of which waited for: 16 -> 19; matrix products, arithmetic and copies ran while one was open for 4% -> 3% of each run, Pallas kernels for 0% -> 0%
where the time goes in v1:
time: 1000 us
  waiting for transfers between devices  612 us (61%)
  starting transfers between devices  110 us (11%)
  blocking collectives  108 us (11%)
  matrix products  94 us (9%)
  local copies, waits for them, and re-layouts  47.7 us (5%)
  between operations  17.3 us (2%)
  other arithmetic  11.3 us (1%)
    psum x1, waiting for transfers between devices, per_device(): grad_middle = lax.psum(local_middle, ('gx', 'gy'))  266 us
    psum x2, waiting for transfers between devices, _hold_scales(): my_data = jax.lax.psum(my_data, tick)  223 us
    psum x1, blocking collectives, per_device(): lax.psum((part_bottom * scale_low).astype(jnp.bfloat16), 'gy')  74.4 us
    reduce_scatter x1, waiting for transfers between devices, per_device(): lax.psum_scatter(partial_sum.astype(jnp.bfloat16), 'gx', scatter_dimensio...  67.3 us
    ppermute x14, starting transfers between devices, extended_2(): lax.ppermute(tail, axis, [(i, (i + 1) % count) for i in range(ends)])  46.2 us
    dot_general x108, matrix products, weight_grad(): lax.dot_general(error_flat, tap_piece(shifted_set, a, b, c, row_count, co...  40.2 us
    ppermute x14, waiting for transfers between devices, extended_2(): lax.ppermute(head, axis, [((i + 1) % count, i) for i in range(ends)])  36.6 us
    all_gather x1, blocking collectives, per_device(): whole_rows = lax.all_gather(col_ext, 'gx', axis=1, tiled=True)  33.5 us
  transfers between devices with their start and end apart: 34, of which 19 were waited for; matrix products, arithmetic and copies ran while one was open for 3% of the time, Pallas kernels for 0%

profile of v1, /device:TPU:4, one launch (start us, length us, event | category | flops | bytes accessed | tf_op | source)
XLA Modules:
  0.0 999.6 jit_solution(15304466553970694971)
XLA Ops:
  11.7 3.1 collective-permute-done.1
  14.8 3.1 collective-permute-start.2
  17.9 2.7 collective-permute-start.3
  20.9 2.6 collective-permute-done.3
  32.6 5.8 collective-permute-start.4
  40.4 3.5 collective-permute-done.5
  44.0 33.5 %all_gather.3 = bf16[64,16,24]{0,2,1:T(8,128)(2,1)S(1)} all-gather(bf16[64,1,24]{0,2,1:T(8,128)(2,1)S(1)} %pad_maximum_fusion.21), channel_id=1, replica_groups=mesh['gx'=16,'gy'=16] {'gx'}, dimensions={1}, use_global_device_ids=true | all-gather | bytes 52224 | tf_op jit(solution)/shard_map/all_gather | solution.py:159
  84.5 6.4 all-to-all-start
  91.0 9.9 all-to-all-done
  106.4 4.2 collective-permute-start.8
  112.6 3.7 collective-permute-done.9
  124.2 3.1 collective-permute-start.10
  128.6 2.7 collective-permute-done.11
  131.5 4.1 collective-permute-start.12
  137.7 3.6 collective-permute-done.13
  156.0 3.4 collective-permute-start.14
  163.9 4.1 collective-permute-start.16
  171.3 2.8 collective-permute-done.17
  209.7 3.1 collective-permute-start.18
  217.2 4.0 collective-permute-start.20
  223.9 3.5 collective-permute-done.21
  256.1 28.9 %all-to-all-start.1 = ((f32[16,1,128]{2,1,0:T(1,128)}), f32[16,1,128]{2,1,0:T(1,128)S(1)}, u32[]{:S(2)}, u32[]{:S(2)}) async-start(f32[16,1,128]{2,1,0:T(1,128)} %reshape.1246), calls=%async_computation.1 | async-start | bytes 16384 | tf_op jit(solution)/shard_map/all_to_all | solution.py:206
  285.9 9.1 all-to-all-done.1
  296.1 4.3 collective-permute-start.22
  303.1 3.1 collective-permute-done.23
  317.9 67.3 %reduce-scatter.2.cloned.1.call-done = bf16[64,1,16]{0,2,1:T(8,128)(2,1)} async-done(((bf16[64,16,16]{0,2,1:T(8,128)(2,1)}), bf16[64,1,16]{0,2,1:T(8,128)(2,1)}) %reduce-scatter.2.cloned.1.call-update) | async-done | bytes 2064 | tf_op jit(solution)/shard_map/reduce_scatter | solution.py:216
  393.1 149.0 %all-reduce.15.cloned.1.call-done = f32[64,864]{0,1:T(8,128)} async-done(((f32[64,864]{0,1:T(8,128)}), f32[64,864]{0,1:T(8,128)}) %all-reduce.15.cloned.1.call-update) | async-done | bytes 221200 | tf_op jit(solution)/shard_map/psum | solution.py:13
  550.5 3.2 collective-permute-done.25
  555.9 5.5 collective-permute-start.27
  561.5 74.4 %psum.37 = bf16[8,1728]{1,0:T(8,128)(2,1)S(1)} all-reduce(bf16[8,1728]{1,0:T(8,128)(2,1)S(1)} %multiply_convert_fusion.3), channel_id=1, replica_groups=mesh['gx'=16,'gy'=16] {'gy'}, use_global_device_ids=true, to_apply=%region_7.8 | all-reduce | flops 13824 | bytes 55296 | tf_op jit(solution)/shard_map/psum | solution.py:219
  648.1 73.5 %all-reduce.17.cloned.1.call-done = f32[64,864]{0,1:T(8,128)} async-done(((f32[64,864]{0,1:T(8,128)}), f32[64,864]{0,1:T(8,128)}) %all-reduce.17.cloned.1.call-update) | async-done | bytes 221200 | tf_op jit(solution)/shard_map/psum | solution.py:13
  723.5 266.3 %all-reduce.19.cloned.1.call-done = (f32[64,5184]{1,0:T(8,128)}, f32[32,2592]{1,0:T(8,128)}) async-done(((f32[64,5184]{1,0:T(8,128)}, f32[32,2592]{1,0:T(8,128)}), (f32[64,5184]{1,0:T(8,128)}, f32[32,2592]{1,0:T(8,128)})) %all-reduce.19.cloned.1.call-update) | async-done | bytes 1658896 | tf_op jit(solution)/shard_map/psum | solution.py:196
  (942 shorter events, 184.7 us)
Async XLA Ops:
  10.4 4.4 collective-permute-start.1
  14.8 6.0 collective-permute-start.2
  17.9 5.5 collective-permute-start.3
  32.6 7.8 collective-permute-start.4
  38.5 5.5 collective-permute-start.5
  84.5 16.4 %all-to-all-start = ((bf16[8,16,16]{2,0,1:T(8,128)(2,1)}), bf16[8,16,16]{2,0,1:T(8,128)(2,1)S(1)}, u32[]{:S(2)}, u32[]{:S(2)}) async-start(bf16[8,16,16]{2,0,1:T(8,128)(2,1)} %copy.83), calls=%async_computation | async-start | bytes 65536 | tf_op jit(solution)/shard_map/all_to_all | solution.py:166
  101.2 3.3 collective-permute-start.6
  103.3 3.2 collective-permute-start.7
  106.4 6.1 collective-permute-start.8
  110.6 5.6 collective-permute-start.9
  124.2 4.5 collective-permute-start.10
  127.3 4.1 collective-permute-start.11
  131.5 6.2 collective-permute-start.12
  135.5 5.7 collective-permute-start.13
  156.0 6.4 collective-permute-start.14
  159.4 4.2 collective-permute-start.15
  163.9 7.4 collective-permute-start.16
  167.9 6.2 collective-permute-start.17
  209.7 5.4 collective-permute-start.18
  212.8 4.2 collective-permute-start.19
  217.2 6.7 collective-permute-start.20
  221.2 6.2 collective-permute-start.21
  256.1 38.8 %all-to-all-start.1 = ((f32[16,1,128]{2,1,0:T(1,128)}), f32[16,1,128]{2,1,0:T(1,128)S(1)}, u32[]{:S(2)}, u32[]{:S(2)}) async-start(f32[16,1,128]{2,1,0:T(1,128)} %reshape.1246), calls=%async_computation.1 | async-start | bytes 16384 | tf_op jit(solution)/shard_map/all_to_all | solution.py:206
  285.1 100.2 %reduce-scatter.2.cloned.1.call-start = ((), (), s32[]{:S(2)}) async-start(), calls=%async_computation.3 | async-start | bytes 69632 | tf_op jit(solution)/shard_map/reduce_scatter | solution.py:216
  296.1 7.0 collective-permute-start.22
  300.4 5.8 collective-permute-start.23
  317.1 225.0 %all-reduce.15.cloned.1.call-start = ((), (), s32[]{:S(2)}) async-start(), calls=%async_computation.4 | async-start | bytes 884736 | tf_op jit(solution)/shard_map/psum | solution.py:13
  390.6 331.0 %all-reduce.17.cloned.1.call-start = ((), (), s32[]{:S(2)}) async-start(), calls=%async_computation.5 | async-start | bytes 884736 | tf_op jit(solution)/shard_map/psum | solution.py:13
  542.1 447.7 %all-reduce.19.cloned.1.call-start = ((), (), s32[]{:S(2)}) async-start(), calls=%async_computation.6 | async-start | bytes 3375104 | tf_op jit(solution)/shard_map/psum | solution.py:196
  549.2 4.6 collective-permute-start.25
  554.0 82.5 %collective-permute-start.26 = (bf16[64,4,8]{2,1,0:T(4,128)(2,1)S(1)}, bf16[64,4,8]{2,1,0:T(4,128)(2,1)S(1)}, u32[]{:S(2)}, u32[]{:S(2)}) collective-permute-start(bf16[64,4,8]{2,1,0:T(4,128)(2,1)S(1)} %get-tuple-element.203), channel_id=1, source_target_pairs={{0,1},{1,2},{2,3},{3,4},{4,5},{5,6},{6,7},{7,8},{8,9},{9,10},{10,1... | collective-permute-start | bytes 12296 | tf_op jit(solution)/shard_map/ppermute | solution.py:28
  555.9 80.5 %collective-permute-start.27 = (bf16[64,4,8]{2,1,0:T(4,128)(2,1)S(1)}, bf16[64,4,8]{2,1,0:T(4,128)(2,1)S(1)}, u32[]{:S(2)}, u32[]{:S(2)}) collective-permute-start(bf16[64,4,8]{2,1,0:T(4,128)(2,1)S(1)} %get-tuple-element.204), channel_id=1, source_target_pairs={{1,0},{2,1},{3,2},{4,3},{5,4},{6,5},{7,6},{8,7},{9,8},{10,9},{11,1... | collective-permute-start | bytes 12296 | tf_op jit(solution)/shard_map/ppermute | solution.py:30
  (145 other events, 4081.6 us)
Sparse Core Ops, SparseCore 0:
  317.2 67.9 reduce-scatter.1
  390.7 151.3 all-reduce.14
  544.7 176.8 all-reduce.16
  727.5 262.2 all-reduce.18
